TPU v7x, 32 devices: a whole 2x2x4 slice. The times are simulated.
32 devices in a mesh: vis: 4 (over y, core), row: 4 (over z), col: 2 (over x).
Axes of the slice: x: 2, y: 2, z: 4, core: 2. Of those that a mesh axis runs over, the one named last changes fastest.
Arguments:
- images: bfloat16 [128, 6400], P(('vis', 'row', 'col')), may hold values from -6 to 6
- counts: int32 [4], replicated, may hold values from 1 to 32, 64 in all
- block_order: int32 [4], replicated, may hold values from 0 to 3, each once
- projector_norm_gain: float32 [6400], replicated, may hold values from 0.1 to 1.9
- proj_first: bfloat16 [6400, 4096], P('vis', ('row', 'col')), may hold values from -0.078125 to 0.078125
- proj_bias: float32 [4096], P(('row', 'col')), may hold values from -3 to 3
- proj_second: bfloat16 [4096, 4096], P(('row', 'col'), 'vis'), may hold values from -0.09375 to 0.09375
- gate_weight: bfloat16 [4096, 16384], P('vis', ('row', 'col')), may hold values from -0.09375 to 0.09375
- up_weight: bfloat16 [4096, 16384], P('vis', ('row', 'col')), may hold values from -0.09375 to 0.09375
- down_weight: bfloat16 [16384, 4096], P(('row', 'col'), 'vis'), may hold values from -0.046875 to 0.046875
- cotangent: bfloat16 [64, 4096], P(('row', 'col'), 'vis'), may hold values from -6 to 6
Outputs:
- block_out: bfloat16 [64, 4096], P(('row', 'col'), 'vis')
- image_slot_gradients: float32 [128, 6400], P(('vis', 'row', 'col'))
- first_grad: float32 [6400, 4096], P('vis', ('row', 'col'))
- second_grad: float32 [4096, 4096], P(('row', 'col'), 'vis')
Inputs may be any that keep to these rules, and one draw needn't show every extreme that they name: Vision device v's live rows are its first counts[v] slots; the counts sum to 64, and some device's slots are all live. `block_order`: each vision device's index once: the order in which the devices' live rows follow one another among the language rows.
All inputs are finite; a program needn't handle non-finite values.
Results may differ from a plain program's by a relative error of at most 0.034.
Values may be sent and summed in bfloat16 or wider, within the bound.
A program may use at most 64 MiB of HBM per device.

v0:
```python
import functools

import jax
import jax.numpy as jnp
from jax import lax
from jax.experimental import pallas as pl
from jax.experimental.pallas import tpu as pltpu
from jax.sharding import PartitionSpec as P


def gelu_parts(pre):
    normal_cdf = 0.5 * (1.0 + jax.scipy.special.erf(pre * 0.7071067811865476))
    density = jnp.exp(-0.5 * pre * pre) * 0.3989422804014327
    return (pre * normal_cdf, normal_cdf + pre * density)


def norm_gradient_pass(gradient_tuple, standardized_input, inverse_scale, projector_norm_gain):
    gain_scaled = gradient_tuple * projector_norm_gain
    return inverse_scale * (
        gain_scaled
        - jnp.mean(gain_scaled, axis=-1, keepdims=True)
        - standardized_input * jnp.mean(gain_scaled * standardized_input, axis=-1, keepdims=True)
    )


def product(left, right):
    return jnp.dot(left, right, preferred_element_type=jnp.float32)


def feed_grads(hidden_grad, gate_sum, up_sum, gate_sigmoid):
    gate_grad = (
        hidden_grad * up_sum * gate_sigmoid * (1.0 + gate_sum * (1.0 - gate_sigmoid))
    ).astype(jnp.bfloat16)
    up_grad = (hidden_grad * gate_sum * gate_sigmoid).astype(jnp.bfloat16)
    return (gate_grad, up_grad)


MESH = pl.DeviceIdType.MESH
BF = jnp.bfloat16
F32 = jnp.float32
ANY = pl.BlockSpec(memory_space=pl.ANY)
VM = pl.BlockSpec(memory_space=pltpu.VMEM)
TILES = 4


def dot_nt(left, right):
    return lax.dot_general(left, right, (((1,), (1,)), ((), ())), preferred_element_type=F32)


def entry_barrier(n, me, coords):
    barrier = pltpu.get_barrier_semaphore()

    def signal(k, carry):
        pl.semaphore_signal(
            barrier, inc=1, device_id=coords(lax.rem(me + k, n)), device_id_type=MESH
        )
        return carry

    lax.fori_loop(1, n, signal, 0)
    return barrier


def spread(src_of, dst, n, me, coords, send_sem, recv_sem, slab=None):
    def body(k, carry):
        p = lax.rem(me + k, n)
        pltpu.make_async_remote_copy(
            src_ref=src_of(p),
            dst_ref=dst.at[me if slab is None else slab],
            send_sem=send_sem,
            recv_sem=recv_sem,
            device_id=coords(p),
            device_id_type=MESH,
        ).start()
        return carry

    lax.fori_loop(1, n, body, 0)


def wait_for(view, sem):
    pltpu.make_async_copy(view, view, sem).wait()


def flat_coords(sizes, p):
    n_vis, _, n_col = sizes
    return (p % n_vis, p // n_vis // n_col, p // n_vis % n_col)


def my_place(sizes):
    n_vis, _, n_col = sizes
    vis, row, col = lax.axis_index("vis"), lax.axis_index("row"), lax.axis_index("col")
    return vis, row, col, (row * n_col + col) * n_vis + vis


def row_places(counts, order, n_vis, per, shape, axis):
    slots = lax.broadcasted_iota(jnp.int32, shape, axis)
    owner = slots // per % n_vis
    offset = slots // (n_vis * per) * per + slots % per
    start_of = jnp.zeros(shape, jnp.int32)
    count_of = jnp.zeros(shape, jnp.int32)
    begin = jnp.int32(0)
    for b in range(n_vis):
        device = order[b]
        live_rows = counts[device]
        start_of = jnp.where(owner == device, begin, start_of)
        count_of = jnp.where(owner == device, live_rows, count_of)
        begin = begin + live_rows
    return jnp.where(offset < count_of, start_of + offset, -1)


def chain_kernel(
    sizes, counts_hbm, order_hbm, images_hbm, gain_hbm, cot_hbm, bias_hbm,
    wf_hbm, ws_hbm, wg_hbm, wu_hbm, wd_hbm,
    block_out, slot_out, packed_out, act_out, hid_out, ig_out,
    counts, order, images, gain, cot, bias, wf, ws, wg, wu, wd,
    blocks, rows_all, cot_all, upstream, slabs, across, column_sums, returned,
    b_part, b_pair, b_ring, b_all, h_part, h_pair, h_ring, h_all,
    d_part, d_pair, d_ring, d_all, f_part, f_pair, f_ring, f_all,
    c_part, c_recv, c_all, e_part, e_recv, e_all, o_part, o_recv,
    slope, inputs, acc, hidden, wsem, gather_sems, return_sems, sems,
):
    n_vis, n_row, n_col = sizes
    group = n_row * n_col
    n_dev = n_vis * group
    vis, row, col, me = my_place(sizes)
    pos = row * n_col + col
    core, ring_at, n_ring = lax.rem(vis, 2), vis // 2, n_vis // 2
    per, vf = blocks.shape[1:]
    rows, dl = upstream.shape
    gr, hr = rows // group, rows // 2
    ffl = wg.shape[1]
    tw = ffl // TILES

    def everyone(p):
        return flat_coords(sizes, p)

    def in_ring(p):
        return (2 * p + core, row, col)

    def in_column(p):
        return (lax.rem(p, n_vis), p // n_vis, col)

    def in_group(p):
        return (vis, p // n_col, p % n_col)

    loads = {}
    for i, (name, src, dst) in enumerate(
        (
            ("images", images_hbm, images), ("gain", gain_hbm, gain), ("cot", cot_hbm, cot),
            ("bias", bias_hbm, bias), ("counts", counts_hbm, counts), ("order", order_hbm, order),
            ("wd", wd_hbm, wd), ("wf", wf_hbm, wf), ("ws", ws_hbm, ws), ("wg", wg_hbm, wg), ("wu", wu_hbm, wu),
        )
    ):
        loads[name] = pltpu.make_async_copy(src, dst, wsem.at[i])
        loads[name].start()
    barrier = entry_barrier(n_dev, me, everyone)

    sent = []

    def pair_of_sems(view):
        idx = 2 * len(sent)
        sent.append((view, sems.at[idx]))
        return sems.at[idx], sems.at[idx + 1]

    def start(src_of, dst, n, at, coords):
        view = dst.at[pl.ds(0, n - 1)]
        send_sem, recv_sem = pair_of_sems(view)
        spread(src_of, dst, n, at, coords, send_sem, recv_sem)
        return lambda: wait_for(view, recv_sem)

    def to_partner(src, dst):
        send_sem, recv_sem = pair_of_sems(dst)
        pltpu.make_async_remote_copy(
            src_ref=src, dst_ref=dst, send_sem=send_sem, recv_sem=recv_sem,
            device_id=(2 * ring_at + 1 - core, row, col), device_id_type=MESH,
        ).start()
        return lambda: wait_for(dst, recv_sem)

    def vis_begin(part, pair):
        return to_partner(part.at[1 - core], pair)

    def vis_middle(arrived, part, pair, ring):
        arrived()
        ring[ring_at] = (part[core].astype(F32) + pair[...].astype(F32)).astype(BF)
        return start(lambda p: ring.at[ring_at], ring, n_ring, ring_at, in_ring)

    def vis_finish(arrived, ring, result):
        arrived()
        value = ring[0].astype(F32)
        for i in range(1, n_ring):
            value = value + ring[i].astype(F32)
        result[core] = value.astype(BF)
        return to_partner(result.at[core], result.at[core])

    def fill(part, value, n, chunk):
        for i in range(n):
            part[i] = value[i * chunk:(i + 1) * chunk].astype(BF)

    def total(recv, part, n, at):
        recv[at] = part[at]
        result = recv[0].astype(F32)
        for i in range(1, n):
            result = result + recv[i].astype(F32)
        return result

    def whole(buf, n):
        return jnp.concatenate([buf[i].astype(F32) for i in range(n)], axis=0)

    loads["images"].wait()
    loads["gain"].wait()
    gain_row = gain[...].reshape(1, gain.shape[0])
    values = images[...].astype(F32)
    centred = values - jnp.mean(values, axis=-1, keepdims=True)
    inverse_scale = lax.rsqrt(jnp.mean(centred * centred, axis=-1, keepdims=True) + 1e-05)
    normed = centred * inverse_scale * gain_row
    for i in range(n_vis):
        blocks[i] = normed[:, i * vf:(i + 1) * vf].astype(BF)
    for name in ("cot", "bias", "counts", "order"):
        loads[name].wait()
    pl.semaphore_wait(barrier, n_dev - 1)
    cot_done = start(lambda p: cot, cot_all, group, pos, in_group)
    mates, own = n_row * n_vis, row * n_vis + vis
    row_steps = sorted(range(n_row), key=lambda k: min(k, n_row - k))
    mates_view = rows_all.at[pl.ds(0, mates - 1)]
    send_sem, _ = pair_of_sems(mates_view)
    spread(
        lambda p: blocks.at[lax.rem(p, n_vis)], rows_all, mates, own, in_column,
        send_sem, gather_sems.at[row], slab=me,
    )
    cot_all[pos] = cot[...]
    rows_all[me] = blocks[vis]
    forward_view = rows_all.at[pl.ds(0, mates * (n_col - 1))]
    forward_send, forward_recv = pair_of_sems(forward_view)

    def forward(k):
        r = lax.rem(row + k, n_row)
        wait_for(rows_all.at[pl.ds(0, n_vis - 1 if k == 0 else n_vis)], gather_sems.at[r])
        chunk = rows_all.at[pl.ds((r * n_col + col) * n_vis, n_vis)]
        for j in range(1, n_col):
            pltpu.make_async_remote_copy(
                src_ref=chunk, dst_ref=chunk, send_sem=forward_send, recv_sem=forward_recv,
                device_id=(vis, row, lax.rem(col + j, n_col)), device_id_type=MESH,
            ).start()

    cot_done()
    upstream[...] = whole(cot_all, group).astype(BF)
    loads["wd"].wait()
    steps_left = list(row_steps)
    for t in range(TILES):
        if steps_left:
            forward(steps_left.pop(0))
        cols = slice(t * tw, (t + 1) * tw)
        value = dot_nt(upstream[...], wd[cols, :])
        for i in range(2):
            h_part[i, :, cols] = value[i * hr:(i + 1) * hr].astype(BF)
    for k in steps_left:
        forward(k)
    h_done = vis_begin(h_part, h_pair)
    n_slots = n_dev * per
    place = row_places(counts, order, n_vis, per, (rows, n_slots), 1)
    pick = jnp.where(place == lax.broadcasted_iota(jnp.int32, (rows, n_slots), 0), 1.0, 0.0).astype(BF)

    loads["wf"].wait()
    wait_for(forward_view, forward_recv)
    packed_out[...] = jnp.dot(
        pick, rows_all[...].reshape(n_slots, vf), preferred_element_type=F32
    ).astype(BF)
    fill(b_part, jnp.dot(packed_out[...], wf[...], preferred_element_type=F32), 2, hr)
    b_done = vis_begin(b_part, b_pair)
    b_done = vis_middle(b_done, b_part, b_pair, b_ring)
    h_done = vis_middle(h_done, h_part, h_pair, h_ring)
    b_done = vis_finish(b_done, b_ring, b_all)
    b_done()
    pre = whole(b_all, 2) + bias[...].reshape(1, bias.shape[0])
    activated, slope_value = gelu_parts(pre)
    slope[...] = slope_value
    hid_out[...] = activated.astype(BF)

    loads["ws"].wait()
    fill(c_part, jnp.dot(hid_out[...], ws[...], preferred_element_type=F32), group, gr)
    c_done = start(lambda p: c_part.at[p], c_recv, group, pos, in_group)
    h_done = vis_finish(h_done, h_ring, h_all)
    c_done()
    c_all[pos] = total(c_recv, c_part, group, pos).astype(BF)
    c_done = start(lambda p: c_all.at[pos], c_all, group, pos, in_group)
    loads["wg"].wait()
    loads["wu"].wait()
    h_done()
    c_done()
    inputs[...] = whole(c_all, group).astype(BF)

    d_done = [None] * TILES
    for t in range(TILES):
        cols = slice(t * tw, (t + 1) * tw)
        for half, weight in enumerate((wg, wu)):
            value = jnp.dot(inputs[...], weight[:, cols], preferred_element_type=F32)
            for i in range(2):
                d_part[t, i, :, half * tw:(half + 1) * tw] = value[i * hr:(i + 1) * hr].astype(BF)
        d_done[t] = vis_begin(d_part.at[t], d_pair.at[t])
        if t > 0:
            d_done[t - 1] = vis_middle(d_done[t - 1], d_part.at[t - 1], d_pair.at[t - 1], d_ring.at[t - 1])
    d_done[-1] = vis_middle(d_done[-1], d_part.at[TILES - 1], d_pair.at[TILES - 1], d_ring.at[TILES - 1])
    d_done[0] = vis_finish(d_done[0], d_ring.at[0], d_all.at[0])
    for t in range(TILES):
        if t + 1 < TILES:
            d_done[t + 1] = vis_finish(d_done[t + 1], d_ring.at[t + 1], d_all.at[t + 1])
        d_done[t]()
        cols = slice(t * tw, (t + 1) * tw)
        both = whole(d_all.at[t], 2)
        gate_sum, up_sum = both[:, :tw], both[:, tw:]
        hidden_grad = jnp.concatenate([h_all[i, :, cols].astype(F32) for i in range(2)], axis=0)
        gate_sigmoid = jax.nn.sigmoid(gate_sum)
        hidden[:, cols] = (gate_sum * gate_sigmoid * up_sum).astype(BF)
        gate_grad, up_grad = feed_grads(hidden_grad, gate_sum, up_sum, gate_sigmoid)
        value = dot_nt(gate_grad, wg[:, cols]) + dot_nt(up_grad, wu[:, cols])
        if t == 0:
            acc[...] = value
        else:
            acc[...] += value
    fill(e_part, acc[...], group, gr)
    e_done = start(lambda p: e_part.at[p], e_recv, group, pos, in_group)

    fill(o_part, jnp.dot(hidden[...], wd[...], preferred_element_type=F32), group, gr)
    e_done()
    e_all[pos] = (total(e_recv, e_part, group, pos) + cot[...].astype(F32)).astype(BF)
    e_done = start(lambda p: e_all.at[pos], e_all, group, pos, in_group)
    o_done = start(lambda p: o_part.at[p], o_recv, group, pos, in_group)
    place = row_places(counts, order, n_vis, per, (n_slots, rows), 0)
    put = jnp.where(place == lax.broadcasted_iota(jnp.int32, (n_slots, rows), 1), 1.0, 0.0).astype(BF)
    e_done()
    ig_out[...] = whole(e_all, group).astype(BF)
    fill(f_part, dot_nt(ig_out[...], ws[...]), 2, hr)
    f_done = vis_begin(f_part, f_pair)
    f_done = vis_middle(f_done, f_part, f_pair, f_ring)
    o_done()
    block_out[...] = (c_all[pos].astype(F32) + total(o_recv, o_part, group, pos)).astype(BF)
    f_done = vis_finish(f_done, f_ring, f_all)
    f_done()
    act_out[...] = (whole(f_all, 2) * slope[...]).astype(BF)

    slot_act = jnp.dot(put, act_out[...], preferred_element_type=F32).astype(BF)
    slabs[...] = dot_nt(slot_act, wf[...]).astype(BF).reshape(n_dev, per, vf)
    across_send, _ = pair_of_sems(slabs.at[pl.ds(0, mates * (n_col - 1))])
    returned_view = returned.at[pl.ds(0, mates - 1)]
    back_send, back_recv = pair_of_sems(returned_view)
    back_steps = row_steps[::-1]
    for k in back_steps:
        r = lax.rem(row + k, n_row)
        for j in range(1, n_col):
            other = lax.rem(col + j, n_col)
            pltpu.make_async_remote_copy(
                src_ref=slabs.at[pl.ds((r * n_col + other) * n_vis, n_vis)],
                dst_ref=across.at[r, col], send_sem=across_send, recv_sem=return_sems.at[r],
                device_id=(vis, row, other), device_id_type=MESH,
            ).start()
    for k in back_steps:
        r = lax.rem(row + k, n_row)
        across[r, col] = slabs[pl.ds((r * n_col + col) * n_vis, n_vis)]
        wait_for(across.at[0, pl.ds(0, n_col - 1)], return_sems.at[r])
        value = across[r, 0].astype(F32)
        for c in range(1, n_col):
            value = value + across[r, c].astype(F32)
        column_sums[r] = value.astype(BF)
        for j in range(1 if k == 0 else 0, n_vis):
            other = lax.rem(vis + j, n_vis)
            pltpu.make_async_remote_copy(
                src_ref=column_sums.at[r, other], dst_ref=returned.at[own],
                send_sem=back_send, recv_sem=back_recv,
                device_id=(other, r, col), device_id_type=MESH,
            ).start()
    returned[own] = column_sums[row, vis]
    wait_for(returned_view, back_recv)
    pieces = []
    for i in range(n_vis):
        value = returned[i].astype(F32)
        for r in range(1, n_row):
            value = value + returned[r * n_vis + i].astype(F32)
        pieces.append(value)
    standardized_input = centred * inverse_scale
    slot_out[...] = norm_gradient_pass(
        jnp.concatenate(pieces, axis=1), standardized_input, inverse_scale, gain_row
    )
    for view, sem in sent:
        wait_for(view, sem)


def vis_buffers(n_vis, lead, half_rows, width):
    return [
        pltpu.VMEM(lead + (2, half_rows, width), BF),
        pltpu.VMEM(lead + (half_rows, width), BF),
        pltpu.VMEM(lead + (n_vis // 2, half_rows, width), BF),
        pltpu.VMEM(lead + (2, half_rows, width), BF),
    ]


def on_device(
    sizes,
    images,
    counts,
    block_order,
    projector_norm_gain,
    proj_first,
    proj_bias,
    proj_second,
    gate_weight,
    up_weight,
    down_weight,
    cotangent,
):
    n_vis, n_row, n_col = sizes
    group_size = n_row * n_col
    n_dev = n_vis * group_size
    per_device = images.shape[0]
    local_rows = cotangent.shape[0]
    rows = local_rows * group_size
    vf, units = proj_first.shape
    dl, ffl = gate_weight.shape
    hr = rows // 2
    by_group = pltpu.VMEM((group_size, local_rows, dl), BF)
    by_device = pltpu.VMEM((n_dev, per_device, vf), BF)
    n_sends = 3 * (3 + TILES) + 5 + 5
    block_out, image_slot_gradients, packed, act_grad, hidden_proj, input_grad = pl.pallas_call(
        functools.partial(chain_kernel, sizes),
        out_shape=(
            jax.ShapeDtypeStruct((local_rows, dl), BF),
            jax.ShapeDtypeStruct(images.shape, F32),
            jax.ShapeDtypeStruct((rows, vf), BF),
            jax.ShapeDtypeStruct((rows, units), BF),
            jax.ShapeDtypeStruct((rows, units), BF),
            jax.ShapeDtypeStruct((rows, dl), BF),
        ),
        in_specs=[ANY] * 11,
        out_specs=(VM,) * 6,
        scratch_shapes=[
            pltpu.SMEM(counts.shape, jnp.int32),
            pltpu.SMEM(block_order.shape, jnp.int32),
            pltpu.VMEM(images.shape, BF),
            pltpu.VMEM(projector_norm_gain.shape, F32),
            pltpu.VMEM(cotangent.shape, BF),
            pltpu.VMEM(proj_bias.shape, F32),
            pltpu.VMEM(proj_first.shape, BF),
            pltpu.VMEM(proj_second.shape, BF),
            pltpu.VMEM(gate_weight.shape, BF),
            pltpu.VMEM(up_weight.shape, BF),
            pltpu.VMEM(down_weight.shape, BF),
            pltpu.VMEM((n_vis, per_device, vf), BF),
            by_device,
            by_group,
            pltpu.VMEM((rows, dl), BF),
            by_device,
            pltpu.VMEM((n_row, n_col, n_vis, per_device, vf), BF),
            pltpu.VMEM((n_row, n_vis, per_device, vf), BF),
            pltpu.VMEM((n_row * n_vis, per_device, vf), BF),
            *vis_buffers(n_vis, (), hr, units),
            *vis_buffers(n_vis, (), hr, ffl),
            *vis_buffers(n_vis, (TILES,), hr, 2 * ffl // TILES),
            *vis_buffers(n_vis, (), hr, units),
            *[by_group] * 8,
            pltpu.VMEM((rows, units), F32),
            pltpu.VMEM((rows, dl), BF),
            pltpu.VMEM((rows, dl), F32),
            pltpu.VMEM((rows, ffl), BF),
            pltpu.SemaphoreType.DMA((11,)),
            pltpu.SemaphoreType.DMA((n_row,)),
            pltpu.SemaphoreType.DMA((n_row,)),
            pltpu.SemaphoreType.DMA((2 * n_sends,)),
        ],
        compiler_params=pltpu.CompilerParams(
            collective_id=0, has_side_effects=True, vmem_limit_bytes=48 << 20
        ),
    )(
        counts, block_order, images, projector_norm_gain, cotangent,
        proj_bias, proj_first, proj_second, gate_weight, up_weight, down_weight,
    )
    second_grad = product(hidden_proj.T, input_grad)
    first_grad = product(packed.T, act_grad)
    return (block_out, image_slot_gradients, first_grad, second_grad)


def solution(mesh):
    in_specs = (
        P(("vis", "row", "col"), None),
        P(),
        P(),
        P(),
        P("vis", ("row", "col")),
        P(("row", "col")),
        P(("row", "col"), "vis"),
        P("vis", ("row", "col")),
        P("vis", ("row", "col")),
        P(("row", "col"), "vis"),
        P(("row", "col"), "vis"),
    )
    out_specs = (
        P(("row", "col"), "vis"),
        P(("vis", "row", "col"), None),
        P("vis", ("row", "col")),
        P(("row", "col"), "vis"),
    )
    sizes = (mesh.shape["vis"], mesh.shape["row"], mesh.shape["col"])
    return jax.shard_map(
        functools.partial(on_device, sizes), mesh=mesh, in_specs=in_specs, out_specs=out_specs, check_vma=False
    )
```

profile of v0, /device:TPU:0, one launch (start us, length us, event | category | flops | bytes accessed | tf_op | source)
XLA Modules:
  0.0 87.5 jit_solution(11473250469374773868)
XLA Ops:
  0.6 0.0 copy-start
  0.6 1.4 %copy-done = bf16[1600,512]{1,0:T(8,128)(2,1)S(1)} copy-done((bf16[1600,512]{1,0:T(8,128)(2,1)S(1)}, bf16[1600,512]{1,0:T(8,128)(2,1)}, u32[]{:S(2)}) %copy-start) | copy-done | bytes 1638424
  2.1 0.0 copy-start.1
  2.1 1.2 %copy-done.1 = bf16[512,1024]{1,0:T(8,128)(2,1)S(1)} copy-done((bf16[512,1024]{1,0:T(8,128)(2,1)S(1)}, bf16[512,1024]{1,0:T(8,128)(2,1)}, u32[]{:S(2)}) %copy-start.1) | copy-done | bytes 1048600
  3.3 0.0 copy-start.2
  3.3 0.8 copy-done.2
  4.1 0.0 copy-start.3
  4.1 0.7 copy-done.3
  4.8 0.0 copy-start.4
  4.8 0.7 copy-done.4
  5.6 0.0 copy-start.5
  5.6 0.7 copy-done.5
  6.2 0.0 copy-start.6
  6.2 0.7 copy-done.6
  6.9 0.0 copy-start.7
  6.9 0.7 copy-done.7
  7.6 74.6 %shard_map.138 = (bf16[8,1024]{1,0:T(8,128)(2,1)S(1)}, f32[4,6400]{1,0:T(4,128)S(1)}, bf16[64,1600]{1,0:T(8,128)(2,1)S(1)}, bf16[64,512]{1,0:T(8,128)(2,1)S(1)},...) custom-call(s32[4]{0:T(128)S(1)} %copy-done.6, s32[4]{0:T(128)S(1)} %copy-done.7, ...), custom_call_target="tpu_custom_call" | custom-call | tf_op jit(solution)/shard_map/pallas_call | solution.py:421
  82.2 2.3 %fusion = f32[1600,512]{1,0:T(8,128)} fusion(bf16[64,1600]{1,0:T(8,128)(2,1)S(1)} %get-tuple-element.12, bf16[64,512]{1,0:T(8,128)(2,1)S(1)} %get-tuple-element.13), kind=kOutput, calls=%fused_computation | convolution fusion | flops 104857600 | bytes 3547136 | tf_op jit(solution)/shard_map/dot_general | solution.py:27
  84.5 1.8 %fusion.1 = f32[512,1024]{1,0:T(8,128)} fusion(bf16[64,512]{1,0:T(8,128)(2,1)S(1)} %get-tuple-element.14, bf16[64,1024]{1,0:T(8,128)(2,1)S(1)} %get-tuple-element.15), kind=kOutput, calls=%fused_computation.1 | convolution fusion | flops 67108864 | bytes 2293760 | tf_op jit(solution)/shard_map/dot_general | solution.py:27
  86.3 0.6 copy.17
  86.9 0.6 copy.18
Async XLA Ops:
  0.6 1.4 %copy-start = (bf16[1600,512]{1,0:T(8,128)(2,1)S(1)}, bf16[1600,512]{1,0:T(8,128)(2,1)}, u32[]{:S(2)}) copy-start(bf16[1600,512]{1,0:T(8,128)(2,1)} %wf_hbm.1) | copy-start | bytes 4915204
  2.1 1.2 %copy-start.1 = (bf16[512,1024]{1,0:T(8,128)(2,1)S(1)}, bf16[512,1024]{1,0:T(8,128)(2,1)}, u32[]{:S(2)}) copy-start(bf16[512,1024]{1,0:T(8,128)(2,1)} %ws_hbm.1) | copy-start | bytes 3145732
  3.3 0.8 copy-start.2
  4.1 0.7 copy-start.3
  4.8 0.7 copy-start.4
  5.6 0.7 copy-start.5
  6.2 0.7 copy-start.6
  6.9 0.7 copy-start.7
where the time goes:
time: 87.9 us; the launch traced here: 87.5 us
  Pallas kernels  74.6 us (85%)
  local copies, waits for them, and re-layouts  8.15 us (9%)
  matrix products  4.1 us (5%)
    pallas_call x1, Pallas kernels, on_device(): pl.pallas_call(functools.partial(chain_kernel, sizes), out_shape=(jax.Sha...  74.6 us
    unnamed x18, local copies, waits for them, and re-layouts  8.15 us
    dot_general x2, matrix products, product(): return jnp.dot(left, right, preferred_element_type=jnp.float32)  4.1 us

commit v1 on v0

--- a/solution.py
+++ b/solution.py
@@ -23,10 +23,6 @@
     )
 
 
-def product(left, right):
-    return jnp.dot(left, right, preferred_element_type=jnp.float32)
-
-
 def feed_grads(hidden_grad, gate_sum, up_sum, gate_sigmoid):
     gate_grad = (
         hidden_grad * up_sum * gate_sigmoid * (1.0 + gate_sum * (1.0 - gate_sigmoid))
@@ -38,9 +34,13 @@
 MESH = pl.DeviceIdType.MESH
 BF = jnp.bfloat16
 F32 = jnp.float32
-ANY = pl.BlockSpec(memory_space=pl.ANY)
+HBM = pl.BlockSpec(memory_space=pltpu.HBM)
 VM = pl.BlockSpec(memory_space=pltpu.VMEM)
 TILES = 4
+
+
+def dot_tn(left, right):
+    return lax.dot_general(left, right, (((0,), (0,)), ((), ())), preferred_element_type=F32)
 
 
 def dot_nt(left, right):
@@ -110,13 +110,13 @@
 def chain_kernel(
     sizes, counts_hbm, order_hbm, images_hbm, gain_hbm, cot_hbm, bias_hbm,
     wf_hbm, ws_hbm, wg_hbm, wu_hbm, wd_hbm,
-    block_out, slot_out, packed_out, act_out, hid_out, ig_out,
+    block_out, slot_out, first_out, second_out,
     counts, order, images, gain, cot, bias, wf, ws, wg, wu, wd,
     blocks, rows_all, cot_all, upstream, slabs, across, column_sums, returned,
     b_part, b_pair, b_ring, b_all, h_part, h_pair, h_ring, h_all,
     d_part, d_pair, d_ring, d_all, f_part, f_pair, f_ring, f_all,
     c_part, c_recv, c_all, e_part, e_recv, e_all, o_part, o_recv,
-    slope, inputs, acc, hidden, wsem, gather_sems, return_sems, sems,
+    packed_out, act_out, hid_out, ig_out, slope, inputs, acc, hidden, wsem, gather_sems, return_sems, sems,
 ):
     n_vis, n_row, n_col = sizes
     group = n_row * n_col
@@ -330,7 +330,10 @@
     ig_out[...] = whole(e_all, group).astype(BF)
     fill(f_part, dot_nt(ig_out[...], ws[...]), 2, hr)
     f_done = vis_begin(f_part, f_pair)
+    half = hid_out.shape[1] // 2
+    second_out[:half] = dot_tn(hid_out[:, :half], ig_out[...])
     f_done = vis_middle(f_done, f_part, f_pair, f_ring)
+    second_out[half:] = dot_tn(hid_out[:, half:], ig_out[...])
     o_done()
     block_out[...] = (c_all[pos].astype(F32) + total(o_recv, o_part, group, pos)).astype(BF)
     f_done = vis_finish(f_done, f_ring, f_all)
@@ -352,6 +355,7 @@
                 dst_ref=across.at[r, col], send_sem=across_send, recv_sem=return_sems.at[r],
                 device_id=(vis, row, other), device_id_type=MESH,
             ).start()
+    first_out[...] = dot_tn(packed_out[...], act_out[...])
     for k in back_steps:
         r = lax.rem(row + k, n_row)
         across[r, col] = slabs[pl.ds((r * n_col + col) * n_vis, n_vis)]
@@ -383,6 +387,15 @@
         wait_for(view, sem)
 
 
+def store_kernel(*refs):
+    sources, targets, sems = refs[:4], refs[4:8], refs[8]
+    copies = [pltpu.make_async_copy(a, b, sems.at[i]) for i, (a, b) in enumerate(zip(sources, targets))]
+    for copy in copies:
+        copy.start()
+    for copy in copies:
+        copy.wait()
+
+
 def vis_buffers(n_vis, lead, half_rows, width):
     return [
         pltpu.VMEM(lead + (2, half_rows, width), BF),
@@ -418,18 +431,16 @@
     by_group = pltpu.VMEM((group_size, local_rows, dl), BF)
     by_device = pltpu.VMEM((n_dev, per_device, vf), BF)
     n_sends = 3 * (3 + TILES) + 5 + 5
-    block_out, image_slot_gradients, packed, act_grad, hidden_proj, input_grad = pl.pallas_call(
+    results = pl.pallas_call(
         functools.partial(chain_kernel, sizes),
         out_shape=(
-            jax.ShapeDtypeStruct((local_rows, dl), BF),
-            jax.ShapeDtypeStruct(images.shape, F32),
-            jax.ShapeDtypeStruct((rows, vf), BF),
-            jax.ShapeDtypeStruct((rows, units), BF),
-            jax.ShapeDtypeStruct((rows, units), BF),
-            jax.ShapeDtypeStruct((rows, dl), BF),
+            pltpu.VMEM((local_rows, dl), BF),
+            pltpu.VMEM(images.shape, F32),
+            pltpu.VMEM((vf, units), F32),
+            pltpu.VMEM((units, dl), F32),
         ),
-        in_specs=[ANY] * 11,
-        out_specs=(VM,) * 6,
+        in_specs=[HBM] * 11,
+        out_specs=(VM,) * 4,
         scratch_shapes=[
             pltpu.SMEM(counts.shape, jnp.int32),
             pltpu.SMEM(block_order.shape, jnp.int32),
@@ -455,6 +466,10 @@
             *vis_buffers(n_vis, (TILES,), hr, 2 * ffl // TILES),
             *vis_buffers(n_vis, (), hr, units),
             *[by_group] * 8,
+            pltpu.VMEM((rows, vf), BF),
+            pltpu.VMEM((rows, units), BF),
+            pltpu.VMEM((rows, units), BF),
+            pltpu.VMEM((rows, dl), BF),
             pltpu.VMEM((rows, units), F32),
             pltpu.VMEM((rows, dl), BF),
             pltpu.VMEM((rows, dl), F32),
@@ -465,15 +480,25 @@
             pltpu.SemaphoreType.DMA((2 * n_sends,)),
         ],
         compiler_params=pltpu.CompilerParams(
-            collective_id=0, has_side_effects=True, vmem_limit_bytes=48 << 20
+            collective_id=0, has_side_effects=True, vmem_limit_bytes=40 << 20
         ),
     )(
-        counts, block_order, images, projector_norm_gain, cotangent,
-        proj_bias, proj_first, proj_second, gate_weight, up_weight, down_weight,
-    )
-    second_grad = product(hidden_proj.T, input_grad)
-    first_grad = product(packed.T, act_grad)
-    return (block_out, image_slot_gradients, first_grad, second_grad)
+        *[
+            pltpu.with_memory_space_constraint(x, pltpu.HBM)
+            for x in (
+                counts, block_order, images, projector_norm_gain, cotangent,
+                proj_bias, proj_first, proj_second, gate_weight, up_weight, down_weight,
+            )
+        ]
+    )
+    return pl.pallas_call(
+        store_kernel,
+        out_shape=tuple(pltpu.HBM(r.shape, r.dtype) for r in results),
+        in_specs=[VM] * 4,
+        out_specs=(HBM,) * 4,
+        scratch_shapes=[pltpu.SemaphoreType.DMA((4,))],
+        compiler_params=pltpu.CompilerParams(vmem_limit_bytes=1 << 20),
+    )(*[pltpu.with_memory_space_constraint(r, pltpu.VMEM) for r in results])
 
 
 def solution(mesh):

time: 87.9 us -> 77.9 us (0.89)
  local copies, waits for them, and re-layouts: 8.15 us -> 0 us
  matrix products: 4.1 us -> 0 us
  Pallas kernels: 74.6 us -> 77.1 us
    unnamed x18 -> x0, local copies, waits for them, and re-layouts: 8.15 us -> none
    dot_general x2 -> x0, matrix products: 4.1 us -> none  [product(): return jnp.dot(left, right, preferred_element_type=jnp.float32)]
    pallas_call x1 -> x2, Pallas kernels: 74.6 us -> 77.1 us  [the longest x1 74.6 us: on_device(): pl.pallas_call(functools.partial(chain_kernel, sizes), out_shape=(pltpu.V...]
where the time goes in v1:
time: 77.9 us; the launch traced here: 77.7 us
  Pallas kernels  77.1 us (99%)
    pallas_call x1, Pallas kernels, on_device(): pl.pallas_call(functools.partial(chain_kernel, sizes), out_shape=(pltpu.V...  74.6 us
    pallas_call x1, Pallas kernels, on_device(): pl.pallas_call(store_kernel, out_shape=tuple((pltpu.HBM(r.shape, r.dtype)...  2.47 us

profile of v1, /device:TPU:0, one launch (start us, length us, event | category | flops | bytes accessed | tf_op | source)
XLA Modules:
  0.0 77.7 jit_solution(16709432428226540043)
XLA Ops:
  0.6 74.6 %shard_map.138 = (bf16[8,1024]{1,0:T(8,128)(2,1)S(1)}, f32[4,6400]{1,0:T(4,128)S(1)}, f32[1600,512]{1,0:T(8,128)S(1)}, f32[512,1024]{1,0:T(8,128)S(1)}) custom-call(s32[4]{0:T(128)} %counts_hbm.1, s32[4]{0:T(128)} %order_hbm.1, bf16[4,6400]{1,0:T(4,128)(2,1)} %images_hbm.1, f32[6400]{0:T(1024)} %gain_hbm.1, bf16[8,1024]{1,0:T(8,128)(2,1)} %cot_hbm.1, ...), custom_call_target="tpu_custom_call" | custom-call | tf_op jit(solution)/shard_map/pallas_call | solution.py:434
  75.3 2.5 %shard_map.139 = (bf16[8,1024]{1,0:T(8,128)(2,1)}, f32[4,6400]{1,0:T(4,128)}, f32[1600,512]{1,0:T(8,128)}, f32[512,1024]{1,0:T(8,128)}) custom-call(bf16[8,1024]{1,0:T(8,128)(2,1)S(1)} %get-tuple-element.8.refs_0_, f32[4,6400]{1,0:T(4,128)S(1)} %get-tuple-element.9.refs_1_, f32[1600,512]{1,0:T(8,128)S(1)} %get-tuple-element.10.refs_2_, ...), custom_call_target="tpu_custom_call" | custom-call | tf_op jit(solution)/shard_map/pallas_call | solution.py:494

commit v2 on v1

--- a/solution.py
+++ b/solution.py
@@ -36,7 +36,7 @@
 F32 = jnp.float32
 HBM = pl.BlockSpec(memory_space=pltpu.HBM)
 VM = pl.BlockSpec(memory_space=pltpu.VMEM)
-TILES = 4
+TILES = 8
 
 
 def dot_tn(left, right):
@@ -47,42 +47,38 @@
     return lax.dot_general(left, right, (((1,), (1,)), ((), ())), preferred_element_type=F32)
 
 
-def entry_barrier(n, me, coords):
+def entry_barrier(devices):
     barrier = pltpu.get_barrier_semaphore()
-
-    def signal(k, carry):
-        pl.semaphore_signal(
-            barrier, inc=1, device_id=coords(lax.rem(me + k, n)), device_id_type=MESH
-        )
-        return carry
-
-    lax.fori_loop(1, n, signal, 0)
+    for device in devices:
+        pl.semaphore_signal(barrier, inc=1, device_id=device, device_id_type=MESH)
     return barrier
 
 
-def spread(src_of, dst, n, me, coords, send_sem, recv_sem, slab=None):
-    def body(k, carry):
-        p = lax.rem(me + k, n)
+def far_first(me, n):
+    upper = 2 * me // n
+    order = []
+    for j in range(n - 1):
+        down = n - 1 - j
+        down = down - (me - down + n) // n
+        up = j + (j - me + n) // n
+        order.append(upper * up + (1 - upper) * down)
+    return order
+
+
+def spread(targets, dst, send_sem, recv_sem):
+    for src, device in targets:
         pltpu.make_async_remote_copy(
-            src_ref=src_of(p),
-            dst_ref=dst.at[me if slab is None else slab],
+            src_ref=src,
+            dst_ref=dst,
             send_sem=send_sem,
             recv_sem=recv_sem,
-            device_id=coords(p),
+            device_id=device,
             device_id_type=MESH,
         ).start()
-        return carry
-
-    lax.fori_loop(1, n, body, 0)
 
 
 def wait_for(view, sem):
     pltpu.make_async_copy(view, view, sem).wait()
-
-
-def flat_coords(sizes, p):
-    n_vis, _, n_col = sizes
-    return (p % n_vis, p // n_vis // n_col, p // n_vis % n_col)
 
 
 def my_place(sizes):
@@ -113,8 +109,8 @@
     block_out, slot_out, first_out, second_out,
     counts, order, images, gain, cot, bias, wf, ws, wg, wu, wd,
     blocks, rows_all, cot_all, upstream, slabs, across, column_sums, returned,
-    b_part, b_pair, b_ring, b_all, h_part, h_pair, h_ring, h_all,
-    d_part, d_pair, d_ring, d_all, f_part, f_pair, f_ring, f_all,
+    b_part, b_recv, h_part, h_pair, h_ring, h_all,
+    d_part, d_pair, d_ring, d_all, f_part, f_recv,
     c_part, c_recv, c_all, e_part, e_recv, e_all, o_part, o_recv,
     packed_out, act_out, hid_out, ig_out, slope, inputs, acc, hidden, wsem, gather_sems, return_sems, sems,
 ):
@@ -130,17 +126,16 @@
     ffl = wg.shape[1]
     tw = ffl // TILES
 
-    def everyone(p):
-        return flat_coords(sizes, p)
-
     def in_ring(p):
         return (2 * p + core, row, col)
 
-    def in_column(p):
-        return (lax.rem(p, n_vis), p // n_vis, col)
-
-    def in_group(p):
-        return (vis, p // n_col, p % n_col)
+    rows_out = far_first(row, n_row)
+    other_cols = [lax.rem(col + j, n_col) for j in range(1, n_col)]
+    other_vis = [
+        (2 * lax.rem(ring_at + k, n_ring) + side) for k in range(1, n_ring) for side in (1 - core, core)
+    ] + [2 * ring_at + 1 - core]
+    group_order = [(r, c) for r in rows_out for c in (*other_cols, col)] + [(row, c) for c in other_cols]
+    mates = [(v, row, col) for v in other_vis] + [(v, r, col) for r in rows_out for v in (*other_vis, vis)]
 
     loads = {}
     for i, (name, src, dst) in enumerate(
@@ -152,7 +147,8 @@
     ):
         loads[name] = pltpu.make_async_copy(src, dst, wsem.at[i])
         loads[name].start()
-    barrier = entry_barrier(n_dev, me, everyone)
+    neighbours = mates + [(vis, r, c) for r in (*rows_out, row) for c in other_cols]
+    barrier = entry_barrier(neighbours)
 
     sent = []
 
@@ -161,11 +157,20 @@
         sent.append((view, sems.at[idx]))
         return sems.at[idx], sems.at[idx + 1]
 
-    def start(src_of, dst, n, at, coords):
+    def start(targets, dst, n, at):
         view = dst.at[pl.ds(0, n - 1)]
         send_sem, recv_sem = pair_of_sems(view)
-        spread(src_of, dst, n, at, coords, send_sem, recv_sem)
+        spread(targets, dst.at[at], send_sem, recv_sem)
         return lambda: wait_for(view, recv_sem)
+
+    def scatter(part, recv):
+        return start([(part.at[r * n_col + c], (vis, r, c)) for r, c in group_order], recv, group, pos)
+
+    def gather(mine, everything):
+        return start([(mine, (vis, r, c)) for r, c in group_order], everything, group, pos)
+
+    def share(part, recv):
+        return start([(part, (v, row, col)) for v in other_vis], recv, n_vis, vis)
 
     def to_partner(src, dst):
         send_sem, recv_sem = pair_of_sems(dst)
@@ -181,7 +186,8 @@
     def vis_middle(arrived, part, pair, ring):
         arrived()
         ring[ring_at] = (part[core].astype(F32) + pair[...].astype(F32)).astype(BF)
-        return start(lambda p: ring.at[ring_at], ring, n_ring, ring_at, in_ring)
+        others = [in_ring(lax.rem(ring_at + k, n_ring)) for k in range(1, n_ring)]
+        return start([(ring.at[ring_at], device) for device in others], ring, n_ring, ring_at)
 
     def vis_finish(arrived, ring, result):
         arrived()
@@ -195,8 +201,8 @@
         for i in range(n):
             part[i] = value[i * chunk:(i + 1) * chunk].astype(BF)
 
-    def total(recv, part, n, at):
-        recv[at] = part[at]
+    def total(recv, own, n, at):
+        recv[at] = own
         result = recv[0].astype(F32)
         for i in range(1, n):
             result = result + recv[i].astype(F32)
@@ -216,45 +222,19 @@
         blocks[i] = normed[:, i * vf:(i + 1) * vf].astype(BF)
     for name in ("cot", "bias", "counts", "order"):
         loads[name].wait()
-    pl.semaphore_wait(barrier, n_dev - 1)
-    cot_done = start(lambda p: cot, cot_all, group, pos, in_group)
-    mates, own = n_row * n_vis, row * n_vis + vis
-    row_steps = sorted(range(n_row), key=lambda k: min(k, n_row - k))
-    mates_view = rows_all.at[pl.ds(0, mates - 1)]
+    pl.semaphore_wait(barrier, len(neighbours))
+    own = row * n_vis + vis
+    mates_view = rows_all.at[pl.ds(0, len(mates))]
     send_sem, _ = pair_of_sems(mates_view)
-    spread(
-        lambda p: blocks.at[lax.rem(p, n_vis)], rows_all, mates, own, in_column,
-        send_sem, gather_sems.at[row], slab=me,
-    )
-    cot_all[pos] = cot[...]
+    spread([(blocks.at[d[0]], d) for d in mates], rows_all.at[me], send_sem, gather_sems.at[row])
     rows_all[me] = blocks[vis]
-    forward_view = rows_all.at[pl.ds(0, mates * (n_col - 1))]
+    forward_view = rows_all.at[pl.ds(0, n_row * n_vis * (n_col - 1))]
     forward_send, forward_recv = pair_of_sems(forward_view)
 
-    def forward(k):
-        r = lax.rem(row + k, n_row)
-        wait_for(rows_all.at[pl.ds(0, n_vis - 1 if k == 0 else n_vis)], gather_sems.at[r])
+    for i, r in enumerate((row, *rows_out[::-1])):
+        wait_for(rows_all.at[pl.ds(0, n_vis - 1 if i == 0 else n_vis)], gather_sems.at[r])
         chunk = rows_all.at[pl.ds((r * n_col + col) * n_vis, n_vis)]
-        for j in range(1, n_col):
-            pltpu.make_async_remote_copy(
-                src_ref=chunk, dst_ref=chunk, send_sem=forward_send, recv_sem=forward_recv,
-                device_id=(vis, row, lax.rem(col + j, n_col)), device_id_type=MESH,
-            ).start()
-
-    cot_done()
-    upstream[...] = whole(cot_all, group).astype(BF)
-    loads["wd"].wait()
-    steps_left = list(row_steps)
-    for t in range(TILES):
-        if steps_left:
-            forward(steps_left.pop(0))
-        cols = slice(t * tw, (t + 1) * tw)
-        value = dot_nt(upstream[...], wd[cols, :])
-        for i in range(2):
-            h_part[i, :, cols] = value[i * hr:(i + 1) * hr].astype(BF)
-    for k in steps_left:
-        forward(k)
-    h_done = vis_begin(h_part, h_pair)
+        spread([(chunk, (vis, row, c)) for c in other_cols], chunk, forward_send, forward_recv)
     n_slots = n_dev * per
     place = row_places(counts, order, n_vis, per, (rows, n_slots), 1)
     pick = jnp.where(place == lax.broadcasted_iota(jnp.int32, (rows, n_slots), 0), 1.0, 0.0).astype(BF)
@@ -264,27 +244,35 @@
     packed_out[...] = jnp.dot(
         pick, rows_all[...].reshape(n_slots, vf), preferred_element_type=F32
     ).astype(BF)
-    fill(b_part, jnp.dot(packed_out[...], wf[...], preferred_element_type=F32), 2, hr)
-    b_done = vis_begin(b_part, b_pair)
-    b_done = vis_middle(b_done, b_part, b_pair, b_ring)
-    h_done = vis_middle(h_done, h_part, h_pair, h_ring)
-    b_done = vis_finish(b_done, b_ring, b_all)
+    b_part[...] = jnp.dot(packed_out[...], wf[...], preferred_element_type=F32).astype(BF)
+    b_done = share(b_part, b_recv)
+    cot_done = gather(cot, cot_all)
+    cot_all[pos] = cot[...]
     b_done()
-    pre = whole(b_all, 2) + bias[...].reshape(1, bias.shape[0])
+    pre = total(b_recv, b_part[...], n_vis, vis) + bias[...].reshape(1, bias.shape[0])
     activated, slope_value = gelu_parts(pre)
     slope[...] = slope_value
     hid_out[...] = activated.astype(BF)
 
     loads["ws"].wait()
     fill(c_part, jnp.dot(hid_out[...], ws[...], preferred_element_type=F32), group, gr)
-    c_done = start(lambda p: c_part.at[p], c_recv, group, pos, in_group)
-    h_done = vis_finish(h_done, h_ring, h_all)
+    c_done = scatter(c_part, c_recv)
+    cot_done()
+    upstream[...] = whole(cot_all, group).astype(BF)
+    loads["wd"].wait()
+    for t in range(TILES):
+        cols = slice(t * tw, (t + 1) * tw)
+        value = dot_nt(upstream[...], wd[cols, :])
+        for i in range(2):
+            h_part[i, :, cols] = value[i * hr:(i + 1) * hr].astype(BF)
+    h_done = vis_begin(h_part, h_pair)
+    h_done = vis_middle(h_done, h_part, h_pair, h_ring)
     c_done()
-    c_all[pos] = total(c_recv, c_part, group, pos).astype(BF)
-    c_done = start(lambda p: c_all.at[pos], c_all, group, pos, in_group)
+    c_all[pos] = total(c_recv, c_part[pos], group, pos).astype(BF)
+    c_done = gather(c_all.at[pos], c_all)
     loads["wg"].wait()
     loads["wu"].wait()
-    h_done()
+    h_done = vis_finish(h_done, h_ring, h_all)
     c_done()
     inputs[...] = whole(c_all, group).astype(BF)
 
@@ -304,6 +292,8 @@
         if t + 1 < TILES:
             d_done[t + 1] = vis_finish(d_done[t + 1], d_ring.at[t + 1], d_all.at[t + 1])
         d_done[t]()
+        if t == 0:
+            h_done()
         cols = slice(t * tw, (t + 1) * tw)
         both = whole(d_all.at[t], 2)
         gate_sum, up_sum = both[:, :tw], both[:, tw:]
@@ -317,60 +307,45 @@
         else:
             acc[...] += value
     fill(e_part, acc[...], group, gr)
-    e_done = start(lambda p: e_part.at[p], e_recv, group, pos, in_group)
-
+    e_done = scatter(e_part, e_recv)
     fill(o_part, jnp.dot(hidden[...], wd[...], preferred_element_type=F32), group, gr)
-    e_done()
-    e_all[pos] = (total(e_recv, e_part, group, pos) + cot[...].astype(F32)).astype(BF)
-    e_done = start(lambda p: e_all.at[pos], e_all, group, pos, in_group)
-    o_done = start(lambda p: o_part.at[p], o_recv, group, pos, in_group)
     place = row_places(counts, order, n_vis, per, (n_slots, rows), 0)
     put = jnp.where(place == lax.broadcasted_iota(jnp.int32, (n_slots, rows), 1), 1.0, 0.0).astype(BF)
     e_done()
+    e_all[pos] = (total(e_recv, e_part[pos], group, pos) + cot[...].astype(F32)).astype(BF)
+    e_done = gather(e_all.at[pos], e_all)
+    e_done()
     ig_out[...] = whole(e_all, group).astype(BF)
-    fill(f_part, dot_nt(ig_out[...], ws[...]), 2, hr)
-    f_done = vis_begin(f_part, f_pair)
-    half = hid_out.shape[1] // 2
-    second_out[:half] = dot_tn(hid_out[:, :half], ig_out[...])
-    f_done = vis_middle(f_done, f_part, f_pair, f_ring)
-    second_out[half:] = dot_tn(hid_out[:, half:], ig_out[...])
-    o_done()
-    block_out[...] = (c_all[pos].astype(F32) + total(o_recv, o_part, group, pos)).astype(BF)
-    f_done = vis_finish(f_done, f_ring, f_all)
+    f_part[...] = dot_nt(ig_out[...], ws[...]).astype(BF)
+    f_done = share(f_part, f_recv)
+    o_done = scatter(o_part, o_recv)
+    second_out[...] = dot_tn(hid_out[...], ig_out[...])
     f_done()
-    act_out[...] = (whole(f_all, 2) * slope[...]).astype(BF)
+    act_out[...] = (total(f_recv, f_part[...], n_vis, vis) * slope[...]).astype(BF)
 
     slot_act = jnp.dot(put, act_out[...], preferred_element_type=F32).astype(BF)
     slabs[...] = dot_nt(slot_act, wf[...]).astype(BF).reshape(n_dev, per, vf)
-    across_send, _ = pair_of_sems(slabs.at[pl.ds(0, mates * (n_col - 1))])
-    returned_view = returned.at[pl.ds(0, mates - 1)]
+    across_send, _ = pair_of_sems(slabs.at[pl.ds(0, n_row * n_vis * (n_col - 1))])
+    returned_view = returned.at[pl.ds(0, n_row * n_vis - 1)]
     back_send, back_recv = pair_of_sems(returned_view)
-    back_steps = row_steps[::-1]
-    for k in back_steps:
-        r = lax.rem(row + k, n_row)
-        for j in range(1, n_col):
-            other = lax.rem(col + j, n_col)
-            pltpu.make_async_remote_copy(
-                src_ref=slabs.at[pl.ds((r * n_col + other) * n_vis, n_vis)],
-                dst_ref=across.at[r, col], send_sem=across_send, recv_sem=return_sems.at[r],
-                device_id=(vis, row, other), device_id_type=MESH,
-            ).start()
+    for r in (*rows_out, row):
+        for c in other_cols:
+            spread(
+                [(slabs.at[pl.ds((r * n_col + c) * n_vis, n_vis)], (vis, row, c))],
+                across.at[r, col], across_send, return_sems.at[r],
+            )
     first_out[...] = dot_tn(packed_out[...], act_out[...])
-    for k in back_steps:
-        r = lax.rem(row + k, n_row)
+    for r in (*rows_out, row):
         across[r, col] = slabs[pl.ds((r * n_col + col) * n_vis, n_vis)]
         wait_for(across.at[0, pl.ds(0, n_col - 1)], return_sems.at[r])
         value = across[r, 0].astype(F32)
         for c in range(1, n_col):
             value = value + across[r, c].astype(F32)
         column_sums[r] = value.astype(BF)
-        for j in range(1 if k == 0 else 0, n_vis):
-            other = lax.rem(vis + j, n_vis)
-            pltpu.make_async_remote_copy(
-                src_ref=column_sums.at[r, other], dst_ref=returned.at[own],
-                send_sem=back_send, recv_sem=back_recv,
-                device_id=(other, r, col), device_id_type=MESH,
-            ).start()
+        targets = other_vis if r is row else (*other_vis, vis)
+        spread([(column_sums.at[r, v], (v, r, col)) for v in targets], returned.at[own], back_send, back_recv)
+    o_done()
+    block_out[...] = (c_all[pos].astype(F32) + total(o_recv, o_part[pos], group, pos)).astype(BF)
     returned[own] = column_sums[row, vis]
     wait_for(returned_view, back_recv)
     pieces = []
@@ -430,7 +405,7 @@
     hr = rows // 2
     by_group = pltpu.VMEM((group_size, local_rows, dl), BF)
     by_device = pltpu.VMEM((n_dev, per_device, vf), BF)
-    n_sends = 3 * (3 + TILES) + 5 + 5
+    n_sends = 3 * (1 + TILES) + 12
     results = pl.pallas_call(
         functools.partial(chain_kernel, sizes),
         out_shape=(
@@ -461,10 +436,12 @@
             pltpu.VMEM((n_row, n_col, n_vis, per_device, vf), BF),
             pltpu.VMEM((n_row, n_vis, per_device, vf), BF),
             pltpu.VMEM((n_row * n_vis, per_device, vf), BF),
-            *vis_buffers(n_vis, (), hr, units),
+            pltpu.VMEM((rows, units), BF),
+            pltpu.VMEM((n_vis, rows, units), BF),
             *vis_buffers(n_vis, (), hr, ffl),
             *vis_buffers(n_vis, (TILES,), hr, 2 * ffl // TILES),
-            *vis_buffers(n_vis, (), hr, units),
+            pltpu.VMEM((rows, units), BF),
+            pltpu.VMEM((n_vis, rows, units), BF),
             *[by_group] * 8,
             pltpu.VMEM((rows, vf), BF),
             pltpu.VMEM((rows, units), BF),

time: 77.9 us -> 68.7 us (0.88)
  Pallas kernels: 77.1 us -> 67.9 us
    pallas_call x1, Pallas kernels: 74.6 us -> 65.5 us  [on_device(): pl.pallas_call(functools.partial(chain_kernel, sizes), out_shape=(pltpu.V...]
where the time goes in v2:
time: 68.7 us; the launch traced here: 68.6 us
  Pallas kernels  67.9 us (99%)
    pallas_call x1, Pallas kernels, on_device(): pl.pallas_call(functools.partial(chain_kernel, sizes), out_shape=(pltpu.V...  65.5 us
    pallas_call x1, Pallas kernels, on_device(): pl.pallas_call(store_kernel, out_shape=tuple((pltpu.HBM(r.shape, r.dtype)...  2.47 us

profile of v2, /device:TPU:0, one launch (start us, length us, event | category | flops | bytes accessed | tf_op | source)
XLA Modules:
  0.0 68.6 jit_solution(9393796552321772506)
XLA Ops:
  0.6 65.5 %shard_map.138 = (bf16[8,1024]{1,0:T(8,128)(2,1)S(1)}, f32[4,6400]{1,0:T(4,128)S(1)}, f32[1600,512]{1,0:T(8,128)S(1)}, f32[512,1024]{1,0:T(8,128)S(1)}) custom-call(s32[4]{0:T(128)} %counts_hbm.1, s32[4]{0:T(128)} %order_hbm.1, bf16[4,6400]{1,0:T(4,128)(2,1)} %images_hbm.1, f32[6400]{0:T(1024)} %gain_hbm.1, bf16[8,1024]{1,0:T(8,128)(2,1)} %cot_hbm.1, ...), custom_call_target="tpu_custom_call" | custom-call | tf_op jit(solution)/shard_map/pallas_call | solution.py:409
  66.1 2.5 %shard_map.139 = (bf16[8,1024]{1,0:T(8,128)(2,1)}, f32[4,6400]{1,0:T(4,128)}, f32[1600,512]{1,0:T(8,128)}, f32[512,1024]{1,0:T(8,128)}) custom-call(bf16[8,1024]{1,0:T(8,128)(2,1)S(1)} %get-tuple-element.8.refs_0_, f32[4,6400]{1,0:T(4,128)S(1)} %get-tuple-element.9.refs_1_, f32[1600,512]{1,0:T(8,128)S(1)} %get-tuple-element.10.refs_2_, ...), custom_call_target="tpu_custom_call" | custom-call | tf_op jit(solution)/shard_map/pallas_call | solution.py:471

commit v3 on v2

--- a/solution.py
+++ b/solution.py
@@ -36,7 +36,10 @@
 F32 = jnp.float32
 HBM = pl.BlockSpec(memory_space=pltpu.HBM)
 VM = pl.BlockSpec(memory_space=pltpu.VMEM)
-TILES = 8
+HALVES = 2
+TILES = 4
+LAG = 2
+AHEAD = 2
 
 
 def dot_tn(left, right):
@@ -87,7 +90,7 @@
     return vis, row, col, (row * n_col + col) * n_vis + vis
 
 
-def row_places(counts, order, n_vis, per, shape, axis):
+def row_places(counts, order, n_vis, per, group, rows, shape, axis):
     slots = lax.broadcasted_iota(jnp.int32, shape, axis)
     owner = slots // per % n_vis
     offset = slots // (n_vis * per) * per + slots % per
@@ -100,7 +103,11 @@
         start_of = jnp.where(owner == device, begin, start_of)
         count_of = jnp.where(owner == device, live_rows, count_of)
         begin = begin + live_rows
-    return jnp.where(offset < count_of, start_of + offset, -1)
+    language = start_of + offset
+    owned = rows // group
+    gr = owned // HALVES
+    working = language % owned // gr * (rows // HALVES) + language // owned * gr + language % gr
+    return jnp.where(offset < count_of, working, -1)
 
 
 def chain_kernel(
@@ -108,7 +115,7 @@
     wf_hbm, ws_hbm, wg_hbm, wu_hbm, wd_hbm,
     block_out, slot_out, first_out, second_out,
     counts, order, images, gain, cot, bias, wf, ws, wg, wu, wd,
-    blocks, rows_all, cot_all, upstream, slabs, across, column_sums, returned,
+    blocks, rows_all, cot_mine, cot_all, upstream, slabs, across, column_sums, returned, direct,
     b_part, b_recv, h_part, h_pair, h_ring, h_all,
     d_part, d_pair, d_ring, d_all, f_part, f_recv,
     c_part, c_recv, c_all, e_part, e_recv, e_all, o_part, o_recv,
@@ -122,7 +129,9 @@
     core, ring_at, n_ring = lax.rem(vis, 2), vis // 2, n_vis // 2
     per, vf = blocks.shape[1:]
     rows, dl = upstream.shape
-    gr, hr = rows // group, rows // 2
+    hr = rows // HALVES
+    gr = hr // group
+    halves = [slice(h * hr, (h + 1) * hr) for h in range(HALVES)]
     ffl = wg.shape[1]
     tw = ffl // TILES
 
@@ -135,6 +144,8 @@
         (2 * lax.rem(ring_at + k, n_ring) + side) for k in range(1, n_ring) for side in (1 - core, core)
     ] + [2 * ring_at + 1 - core]
     group_order = [(r, c) for r in rows_out for c in (*other_cols, col)] + [(row, c) for c in other_cols]
+    all_vis = (*other_vis, vis)
+    row_mates = [(v, row, c) for c in other_cols for v in all_vis]
     mates = [(v, row, col) for v in other_vis] + [(v, r, col) for r in rows_out for v in (*other_vis, vis)]
 
     loads = {}
@@ -147,7 +158,7 @@
     ):
         loads[name] = pltpu.make_async_copy(src, dst, wsem.at[i])
         loads[name].start()
-    neighbours = mates + [(vis, r, c) for r in (*rows_out, row) for c in other_cols]
+    neighbours = mates + [(vis, r, c) for r in rows_out for c in other_cols] + row_mates
     barrier = entry_barrier(neighbours)
 
     sent = []
@@ -197,9 +208,8 @@
         result[core] = value.astype(BF)
         return to_partner(result.at[core], result.at[core])
 
-    def fill(part, value, n, chunk):
-        for i in range(n):
-            part[i] = value[i * chunk:(i + 1) * chunk].astype(BF)
+    def by_owner(value):
+        return value.astype(BF).reshape(group, gr, value.shape[1])
 
     def total(recv, own, n, at):
         recv[at] = own
@@ -227,126 +237,167 @@
     mates_view = rows_all.at[pl.ds(0, len(mates))]
     send_sem, _ = pair_of_sems(mates_view)
     spread([(blocks.at[d[0]], d) for d in mates], rows_all.at[me], send_sem, gather_sems.at[row])
-    rows_all[me] = blocks[vis]
     forward_view = rows_all.at[pl.ds(0, n_row * n_vis * (n_col - 1))]
     forward_send, forward_recv = pair_of_sems(forward_view)
-
-    for i, r in enumerate((row, *rows_out[::-1])):
-        wait_for(rows_all.at[pl.ds(0, n_vis - 1 if i == 0 else n_vis)], gather_sems.at[r])
+    spread([(blocks.at[v], (v, row, c)) for c in other_cols for v in all_vis], rows_all.at[me], forward_send, forward_recv)
+    rows_all[me] = blocks[vis]
+    for r in rows_out[::-1]:
+        wait_for(rows_all.at[pl.ds(0, n_vis)], gather_sems.at[r])
         chunk = rows_all.at[pl.ds((r * n_col + col) * n_vis, n_vis)]
         spread([(chunk, (vis, row, c)) for c in other_cols], chunk, forward_send, forward_recv)
     n_slots = n_dev * per
-    place = row_places(counts, order, n_vis, per, (rows, n_slots), 1)
+    place = row_places(counts, order, n_vis, per, group, rows, (rows, n_slots), 1)
     pick = jnp.where(place == lax.broadcasted_iota(jnp.int32, (rows, n_slots), 0), 1.0, 0.0).astype(BF)
 
     loads["wf"].wait()
+    wait_for(rows_all.at[pl.ds(0, n_vis - 1)], gather_sems.at[row])
     wait_for(forward_view, forward_recv)
     packed_out[...] = jnp.dot(
         pick, rows_all[...].reshape(n_slots, vf), preferred_element_type=F32
     ).astype(BF)
-    b_part[...] = jnp.dot(packed_out[...], wf[...], preferred_element_type=F32).astype(BF)
-    b_done = share(b_part, b_recv)
-    cot_done = gather(cot, cot_all)
-    cot_all[pos] = cot[...]
-    b_done()
-    pre = total(b_recv, b_part[...], n_vis, vis) + bias[...].reshape(1, bias.shape[0])
-    activated, slope_value = gelu_parts(pre)
-    slope[...] = slope_value
-    hid_out[...] = activated.astype(BF)
-
+    b_done = []
+    for h, half in enumerate(halves):
+        b_part[h] = jnp.dot(packed_out[half], wf[...], preferred_element_type=F32).astype(BF)
+        b_done.append(share(b_part.at[h], b_recv.at[h]))
+    cot_mine[...] = cot[...].reshape(HALVES, gr, dl)
+    cot_done = gather(cot_mine, cot_all)
+    cot_all[pos] = cot_mine[...]
     loads["ws"].wait()
-    fill(c_part, jnp.dot(hid_out[...], ws[...], preferred_element_type=F32), group, gr)
-    c_done = scatter(c_part, c_recv)
+    c_done = []
+    for h, half in enumerate(halves):
+        b_done[h]()
+        pre = total(b_recv.at[h], b_part[h], n_vis, vis) + bias[...].reshape(1, bias.shape[0])
+        activated, slope_value = gelu_parts(pre)
+        slope[half] = slope_value
+        hid_out[half] = activated.astype(BF)
+        c_part[h] = by_owner(jnp.dot(hid_out[half], ws[...], preferred_element_type=F32))
+        c_done.append(scatter(c_part.at[h], c_recv.at[h]))
+
     cot_done()
-    upstream[...] = whole(cot_all, group).astype(BF)
+    for h, half in enumerate(halves):
+        upstream[half] = cot_all[:, h].reshape(hr, dl)
     loads["wd"].wait()
-    for t in range(TILES):
-        cols = slice(t * tw, (t + 1) * tw)
+    mid = rows // 2
+    hw = ffl // 8
+    for t in range(8):
+        cols = slice(t * hw, (t + 1) * hw)
         value = dot_nt(upstream[...], wd[cols, :])
         for i in range(2):
-            h_part[i, :, cols] = value[i * hr:(i + 1) * hr].astype(BF)
+            h_part[i, :, cols] = value[i * mid:(i + 1) * mid].astype(BF)
     h_done = vis_begin(h_part, h_pair)
     h_done = vis_middle(h_done, h_part, h_pair, h_ring)
-    c_done()
-    c_all[pos] = total(c_recv, c_part[pos], group, pos).astype(BF)
-    c_done = gather(c_all.at[pos], c_all)
+    for h in range(HALVES):
+        c_done[h]()
+        c_all[h, pos] = total(c_recv.at[h], c_part[h, pos], group, pos).astype(BF)
+        c_done[h] = gather(c_all.at[h, pos], c_all.at[h])
     loads["wg"].wait()
     loads["wu"].wait()
     h_done = vis_finish(h_done, h_ring, h_all)
-    c_done()
-    inputs[...] = whole(c_all, group).astype(BF)
-
-    d_done = [None] * TILES
-    for t in range(TILES):
+
+    steps = [(h, t) for h in range(HALVES) for t in range(TILES)]
+    d_done = {}
+    hc = hr // 2
+
+    def d_middle(k):
+        d_done[k] = vis_middle(d_done[k], d_part.at[k], d_pair.at[k], d_ring.at[k])
+
+    def d_finish(k):
+        d_done[k] = vis_finish(d_done[k], d_ring.at[k], d_all.at[k])
+
+    for i, (h, t) in enumerate(steps):
+        if t == 0:
+            c_done[h]()
+            inputs[halves[h]] = c_all[h].reshape(hr, dl)
         cols = slice(t * tw, (t + 1) * tw)
-        for half, weight in enumerate((wg, wu)):
-            value = jnp.dot(inputs[...], weight[:, cols], preferred_element_type=F32)
-            for i in range(2):
-                d_part[t, i, :, half * tw:(half + 1) * tw] = value[i * hr:(i + 1) * hr].astype(BF)
-        d_done[t] = vis_begin(d_part.at[t], d_pair.at[t])
-        if t > 0:
-            d_done[t - 1] = vis_middle(d_done[t - 1], d_part.at[t - 1], d_pair.at[t - 1], d_ring.at[t - 1])
-    d_done[-1] = vis_middle(d_done[-1], d_part.at[TILES - 1], d_pair.at[TILES - 1], d_ring.at[TILES - 1])
-    d_done[0] = vis_finish(d_done[0], d_ring.at[0], d_all.at[0])
-    for t in range(TILES):
-        if t + 1 < TILES:
-            d_done[t + 1] = vis_finish(d_done[t + 1], d_ring.at[t + 1], d_all.at[t + 1])
-        d_done[t]()
-        if t == 0:
-            h_done()
+        for part, weight in enumerate((wg, wu)):
+            value = jnp.dot(inputs[halves[h]], weight[:, cols], preferred_element_type=F32)
+            for k in range(2):
+                d_part[h, t, k, :, part * tw:(part + 1) * tw] = value[k * hc:(k + 1) * hc].astype(BF)
+        d_done[h, t] = vis_begin(d_part.at[h, t], d_pair.at[h, t])
+        if i >= LAG:
+            d_middle(steps[i - LAG])
+    for k in steps[-LAG:]:
+        d_middle(k)
+    for k in steps[:AHEAD]:
+        d_finish(k)
+    h_done()
+    e_done = []
+    for i, (h, t) in enumerate(steps):
+        if i + AHEAD < len(steps):
+            d_finish(steps[i + AHEAD])
+        d_done[h, t]()
         cols = slice(t * tw, (t + 1) * tw)
-        both = whole(d_all.at[t], 2)
+        both = whole(d_all.at[h, t], 2)
         gate_sum, up_sum = both[:, :tw], both[:, tw:]
-        hidden_grad = jnp.concatenate([h_all[i, :, cols].astype(F32) for i in range(2)], axis=0)
+        hidden_grad = whole(h_all.at[:, :, cols], 2) if HALVES == 1 else h_all[h, :, cols].astype(F32)
         gate_sigmoid = jax.nn.sigmoid(gate_sum)
-        hidden[:, cols] = (gate_sum * gate_sigmoid * up_sum).astype(BF)
+        hidden[halves[h], cols] = (gate_sum * gate_sigmoid * up_sum).astype(BF)
         gate_grad, up_grad = feed_grads(hidden_grad, gate_sum, up_sum, gate_sigmoid)
         value = dot_nt(gate_grad, wg[:, cols]) + dot_nt(up_grad, wu[:, cols])
         if t == 0:
             acc[...] = value
+        elif t < TILES - 1:
+            acc[...] += value
         else:
-            acc[...] += value
-    fill(e_part, acc[...], group, gr)
-    e_done = scatter(e_part, e_recv)
-    fill(o_part, jnp.dot(hidden[...], wd[...], preferred_element_type=F32), group, gr)
-    place = row_places(counts, order, n_vis, per, (n_slots, rows), 0)
+            e_part[h] = by_owner(acc[...] + value)
+            e_done.append(scatter(e_part.at[h], e_recv.at[h]))
+    value = jnp.dot(hidden[...], wd[...], preferred_element_type=F32)
+    for h, half in enumerate(halves):
+        o_part[:, h] = by_owner(value[half])
+    place = row_places(counts, order, n_vis, per, group, rows, (n_slots, rows), 0)
     put = jnp.where(place == lax.broadcasted_iota(jnp.int32, (n_slots, rows), 1), 1.0, 0.0).astype(BF)
-    e_done()
-    e_all[pos] = (total(e_recv, e_part[pos], group, pos) + cot[...].astype(F32)).astype(BF)
-    e_done = gather(e_all.at[pos], e_all)
-    e_done()
-    ig_out[...] = whole(e_all, group).astype(BF)
-    f_part[...] = dot_nt(ig_out[...], ws[...]).astype(BF)
-    f_done = share(f_part, f_recv)
+    for h in range(HALVES):
+        e_done[h]()
+        e_all[h, pos] = (total(e_recv.at[h], e_part[h, pos], group, pos) + cot_mine[h].astype(F32)).astype(BF)
+        e_done[h] = gather(e_all.at[h, pos], e_all.at[h])
+    f_done = []
+    for h, half in enumerate(halves):
+        e_done[h]()
+        ig_out[half] = e_all[h].reshape(hr, dl)
+        f_part[h] = dot_nt(ig_out[half], ws[...]).astype(BF)
+        f_done.append(share(f_part.at[h], f_recv.at[h]))
     o_done = scatter(o_part, o_recv)
     second_out[...] = dot_tn(hid_out[...], ig_out[...])
-    f_done()
-    act_out[...] = (total(f_recv, f_part[...], n_vis, vis) * slope[...]).astype(BF)
+    for h, half in enumerate(halves):
+        f_done[h]()
+        act_out[half] = (total(f_recv.at[h], f_part[h], n_vis, vis) * slope[half]).astype(BF)
 
     slot_act = jnp.dot(put, act_out[...], preferred_element_type=F32).astype(BF)
     slabs[...] = dot_nt(slot_act, wf[...]).astype(BF).reshape(n_dev, per, vf)
-    across_send, _ = pair_of_sems(slabs.at[pl.ds(0, n_row * n_vis * (n_col - 1))])
-    returned_view = returned.at[pl.ds(0, n_row * n_vis - 1)]
+    across_send, _ = pair_of_sems(slabs.at[pl.ds(0, (n_row - 1) * n_vis * (n_col - 1))])
+    direct_view = direct.at[pl.ds(0, n_vis * n_col - 1)]
+    direct_send, direct_recv = pair_of_sems(direct_view)
+    returned_view = returned.at[pl.ds(0, (n_row - 1) * n_vis)]
     back_send, back_recv = pair_of_sems(returned_view)
-    for r in (*rows_out, row):
+    for r in rows_out:
         for c in other_cols:
             spread(
                 [(slabs.at[pl.ds((r * n_col + c) * n_vis, n_vis)], (vis, row, c))],
                 across.at[r, col], across_send, return_sems.at[r],
             )
+    spread(
+        [(slabs.at[(row * n_col + c) * n_vis + v], (v, row, c)) for v, _, c in row_mates + mates[:n_vis - 1]],
+        direct.at[col * n_vis + vis], direct_send, direct_recv,
+    )
     first_out[...] = dot_tn(packed_out[...], act_out[...])
-    for r in (*rows_out, row):
+    for r in rows_out:
         across[r, col] = slabs[pl.ds((r * n_col + col) * n_vis, n_vis)]
         wait_for(across.at[0, pl.ds(0, n_col - 1)], return_sems.at[r])
         value = across[r, 0].astype(F32)
         for c in range(1, n_col):
             value = value + across[r, c].astype(F32)
         column_sums[r] = value.astype(BF)
-        targets = other_vis if r is row else (*other_vis, vis)
-        spread([(column_sums.at[r, v], (v, r, col)) for v in targets], returned.at[own], back_send, back_recv)
+        spread([(column_sums.at[r, v], (v, r, col)) for v in all_vis], returned.at[own], back_send, back_recv)
     o_done()
-    block_out[...] = (c_all[pos].astype(F32) + total(o_recv, o_part[pos], group, pos)).astype(BF)
-    returned[own] = column_sums[row, vis]
+    o_sum = total(o_recv, o_part[pos], group, pos)
+    block_out[...] = jnp.concatenate([o_sum[h] + c_all[h, pos].astype(F32) for h in range(HALVES)], axis=0).astype(BF)
+    direct[col * n_vis + vis] = slabs[me]
+    wait_for(direct_view, direct_recv)
+    for i in range(n_vis):
+        value = direct[i].astype(F32)
+        for c in range(1, n_col):
+            value = value + direct[c * n_vis + i].astype(F32)
+        returned[row * n_vis + i] = value.astype(BF)
     wait_for(returned_view, back_recv)
     pieces = []
     for i in range(n_vis):
@@ -402,10 +453,12 @@
     rows = local_rows * group_size
     vf, units = proj_first.shape
     dl, ffl = gate_weight.shape
-    hr = rows // 2
-    by_group = pltpu.VMEM((group_size, local_rows, dl), BF)
+    hr = rows // HALVES
+    gr = local_rows // HALVES
+    by_group = pltpu.VMEM((HALVES, group_size, gr, dl), BF)
+    owned_halves = pltpu.VMEM((group_size, HALVES, gr, dl), BF)
     by_device = pltpu.VMEM((n_dev, per_device, vf), BF)
-    n_sends = 3 * (1 + TILES) + 12
+    n_sends = 3 * (1 + HALVES * TILES) + 6 * HALVES + 7
     results = pl.pallas_call(
         functools.partial(chain_kernel, sizes),
         out_shape=(
@@ -430,26 +483,30 @@
             pltpu.VMEM(down_weight.shape, BF),
             pltpu.VMEM((n_vis, per_device, vf), BF),
             by_device,
-            by_group,
+            pltpu.VMEM((HALVES, gr, dl), BF),
+            owned_halves,
             pltpu.VMEM((rows, dl), BF),
             by_device,
             pltpu.VMEM((n_row, n_col, n_vis, per_device, vf), BF),
             pltpu.VMEM((n_row, n_vis, per_device, vf), BF),
             pltpu.VMEM((n_row * n_vis, per_device, vf), BF),
-            pltpu.VMEM((rows, units), BF),
-            pltpu.VMEM((n_vis, rows, units), BF),
-            *vis_buffers(n_vis, (), hr, ffl),
-            *vis_buffers(n_vis, (TILES,), hr, 2 * ffl // TILES),
-            pltpu.VMEM((rows, units), BF),
-            pltpu.VMEM((n_vis, rows, units), BF),
-            *[by_group] * 8,
+            pltpu.VMEM((n_col * n_vis, per_device, vf), BF),
+            pltpu.VMEM((HALVES, hr, units), BF),
+            pltpu.VMEM((HALVES, n_vis, hr, units), BF),
+            *vis_buffers(n_vis, (), rows // 2, ffl),
+            *vis_buffers(n_vis, (HALVES, TILES), hr // 2, 2 * ffl // TILES),
+            pltpu.VMEM((HALVES, hr, units), BF),
+            pltpu.VMEM((HALVES, n_vis, hr, units), BF),
+            *[by_group] * 6,
+            owned_halves,
+            owned_halves,
             pltpu.VMEM((rows, vf), BF),
             pltpu.VMEM((rows, units), BF),
             pltpu.VMEM((rows, units), BF),
             pltpu.VMEM((rows, dl), BF),
             pltpu.VMEM((rows, units), F32),
             pltpu.VMEM((rows, dl), BF),
-            pltpu.VMEM((rows, dl), F32),
+            pltpu.VMEM((hr, dl), F32),
             pltpu.VMEM((rows, ffl), BF),
             pltpu.SemaphoreType.DMA((11,)),
             pltpu.SemaphoreType.DMA((n_row,)),

time: 68.7 us -> 66.9 us (0.974)
  Pallas kernels: 67.9 us -> 66.1 us
    pallas_call x1, Pallas kernels: 65.5 us -> 63.6 us  [on_device(): pl.pallas_call(functools.partial(chain_kernel, sizes), out_shape=(pltpu.V...]
where the time goes in v3:
time: 66.9 us; the launch traced here: 66.7 us
  Pallas kernels  66.1 us (99%)
    pallas_call x1, Pallas kernels, on_device(): pl.pallas_call(functools.partial(chain_kernel, sizes), out_shape=(pltpu.V...  63.6 us
    pallas_call x1, Pallas kernels, on_device(): pl.pallas_call(store_kernel, out_shape=tuple((pltpu.HBM(r.shape, r.dtype)...  2.47 us

profile of v3, /device:TPU:0, one launch (start us, length us, event | category | flops | bytes accessed | tf_op | source)
XLA Modules:
  0.0 66.7 jit_solution(13206472288355052939)
XLA Ops:
  0.6 63.6 %shard_map.138 = (bf16[8,1024]{1,0:T(8,128)(2,1)S(1)}, f32[4,6400]{1,0:T(4,128)S(1)}, f32[1600,512]{1,0:T(8,128)S(1)}, f32[512,1024]{1,0:T(8,128)S(1)}) custom-call(s32[4]{0:T(128)} %counts_hbm.1, s32[4]{0:T(128)} %order_hbm.1, bf16[4,6400]{1,0:T(4,128)(2,1)} %images_hbm.1, f32[6400]{0:T(1024)} %gain_hbm.1, bf16[8,1024]{1,0:T(8,128)(2,1)} %cot_hbm.1, ...), custom_call_target="tpu_custom_call" | custom-call | tf_op jit(solution)/shard_map/pallas_call | solution.py:462
  64.3 2.5 %shard_map.139 = (bf16[8,1024]{1,0:T(8,128)(2,1)}, f32[4,6400]{1,0:T(4,128)}, f32[1600,512]{1,0:T(8,128)}, f32[512,1024]{1,0:T(8,128)}) custom-call(bf16[8,1024]{1,0:T(8,128)(2,1)S(1)} %get-tuple-element.8.refs_0_, f32[4,6400]{1,0:T(4,128)S(1)} %get-tuple-element.9.refs_1_, f32[1600,512]{1,0:T(8,128)S(1)} %get-tuple-element.10.refs_2_, ...), custom_call_target="tpu_custom_call" | custom-call | tf_op jit(solution)/shard_map/pallas_call | solution.py:528

commit v4 on v3

--- a/solution.py
+++ b/solution.py
@@ -40,6 +40,11 @@
 TILES = 4
 LAG = 2
 AHEAD = 2
+FLIPS = 8
+
+
+def product(left, right):
+    return jnp.dot(left, right, preferred_element_type=F32)
 
 
 def dot_tn(left, right):
@@ -114,7 +119,7 @@
     sizes, counts_hbm, order_hbm, images_hbm, gain_hbm, cot_hbm, bias_hbm,
     wf_hbm, ws_hbm, wg_hbm, wu_hbm, wd_hbm,
     block_out, slot_out, first_out, second_out,
-    counts, order, images, gain, cot, bias, wf, ws, wg, wu, wd,
+    counts, order, images, gain, cot, bias, wf, ws, wg, wu, wd, wgt, wut, wst, wft,
     blocks, rows_all, cot_mine, cot_all, upstream, slabs, across, column_sums, returned, direct,
     b_part, b_recv, h_part, h_pair, h_ring, h_all,
     d_part, d_pair, d_ring, d_all, f_part, f_recv,
@@ -146,7 +151,7 @@
     group_order = [(r, c) for r in rows_out for c in (*other_cols, col)] + [(row, c) for c in other_cols]
     all_vis = (*other_vis, vis)
     row_mates = [(v, row, c) for c in other_cols for v in all_vis]
-    mates = [(v, row, col) for v in other_vis] + [(v, r, col) for r in rows_out for v in (*other_vis, vis)]
+    mates = [(v, row, col) for v in other_vis] + [(v, r, col) for r in rows_out[::-1] for v in (*other_vis, vis)]
 
     loads = {}
     for i, (name, src, dst) in enumerate(
@@ -241,10 +246,19 @@
     forward_send, forward_recv = pair_of_sems(forward_view)
     spread([(blocks.at[v], (v, row, c)) for c in other_cols for v in all_vis], rows_all.at[me], forward_send, forward_recv)
     rows_all[me] = blocks[vis]
-    for r in rows_out[::-1]:
+    flips = [(a, b, slice(t * ffl // FLIPS, (t + 1) * ffl // FLIPS)) for t in range(FLIPS) for a, b in ((wg, wgt), (wu, wut))]
+    flips_each = len(flips) // n_row
+    for i, r in enumerate(rows_out[::-1]):
         wait_for(rows_all.at[pl.ds(0, n_vis)], gather_sems.at[r])
         chunk = rows_all.at[pl.ds((r * n_col + col) * n_vis, n_vis)]
         spread([(chunk, (vis, row, c)) for c in other_cols], chunk, forward_send, forward_recv)
+        if i == 0:
+            loads["wg"].wait()
+            loads["wu"].wait()
+        for source, target, band in flips[i * flips_each:(i + 1) * flips_each]:
+            target[band, :] = source[:, band].T
+    for source, target, band in flips[(n_row - 1) * flips_each:]:
+        target[band, :] = source[:, band].T
     n_slots = n_dev * per
     place = row_places(counts, order, n_vis, per, group, rows, (rows, n_slots), 1)
     pick = jnp.where(place == lax.broadcasted_iota(jnp.int32, (rows, n_slots), 0), 1.0, 0.0).astype(BF)
@@ -290,8 +304,8 @@
         c_done[h]()
         c_all[h, pos] = total(c_recv.at[h], c_part[h, pos], group, pos).astype(BF)
         c_done[h] = gather(c_all.at[h, pos], c_all.at[h])
-    loads["wg"].wait()
-    loads["wu"].wait()
+    wst[...] = ws[...].T
+    wft[...] = wf[...].T
     h_done = vis_finish(h_done, h_ring, h_all)
 
     steps = [(h, t) for h in range(HALVES) for t in range(TILES)]
@@ -333,7 +347,7 @@
         gate_sigmoid = jax.nn.sigmoid(gate_sum)
         hidden[halves[h], cols] = (gate_sum * gate_sigmoid * up_sum).astype(BF)
         gate_grad, up_grad = feed_grads(hidden_grad, gate_sum, up_sum, gate_sigmoid)
-        value = dot_nt(gate_grad, wg[:, cols]) + dot_nt(up_grad, wu[:, cols])
+        value = product(gate_grad, wgt[cols, :]) + product(up_grad, wut[cols, :])
         if t == 0:
             acc[...] = value
         elif t < TILES - 1:
@@ -354,7 +368,7 @@
     for h, half in enumerate(halves):
         e_done[h]()
         ig_out[half] = e_all[h].reshape(hr, dl)
-        f_part[h] = dot_nt(ig_out[half], ws[...]).astype(BF)
+        f_part[h] = product(ig_out[half], wst[...]).astype(BF)
         f_done.append(share(f_part.at[h], f_recv.at[h]))
     o_done = scatter(o_part, o_recv)
     second_out[...] = dot_tn(hid_out[...], ig_out[...])
@@ -363,7 +377,7 @@
         act_out[half] = (total(f_recv.at[h], f_part[h], n_vis, vis) * slope[half]).astype(BF)
 
     slot_act = jnp.dot(put, act_out[...], preferred_element_type=F32).astype(BF)
-    slabs[...] = dot_nt(slot_act, wf[...]).astype(BF).reshape(n_dev, per, vf)
+    slabs[...] = product(slot_act, wft[...]).astype(BF).reshape(n_dev, per, vf)
     across_send, _ = pair_of_sems(slabs.at[pl.ds(0, (n_row - 1) * n_vis * (n_col - 1))])
     direct_view = direct.at[pl.ds(0, n_vis * n_col - 1)]
     direct_send, direct_recv = pair_of_sems(direct_view)
@@ -481,6 +495,10 @@
             pltpu.VMEM(gate_weight.shape, BF),
             pltpu.VMEM(up_weight.shape, BF),
             pltpu.VMEM(down_weight.shape, BF),
+            pltpu.VMEM((ffl, dl), BF),
+            pltpu.VMEM((ffl, dl), BF),
+            pltpu.VMEM((dl, units), BF),
+            pltpu.VMEM((units, vf), BF),
             pltpu.VMEM((n_vis, per_device, vf), BF),
             by_device,
             pltpu.VMEM((HALVES, gr, dl), BF),
@@ -514,7 +532,7 @@
             pltpu.SemaphoreType.DMA((2 * n_sends,)),
         ],
         compiler_params=pltpu.CompilerParams(
-            collective_id=0, has_side_effects=True, vmem_limit_bytes=40 << 20
+            collective_id=0, has_side_effects=True, vmem_limit_bytes=48 << 20
         ),
     )(
         *[

time: 66.9 us -> 65.2 us (0.975)
  Pallas kernels: 66.1 us -> 64.4 us
    pallas_call x1, Pallas kernels: 63.6 us -> 61.9 us  [on_device(): pl.pallas_call(functools.partial(chain_kernel, sizes), out_shape=(pltpu.V...]
where the time goes in v4:
time: 65.2 us; the launch traced here: 65 us
  Pallas kernels  64.4 us (99%)
    pallas_call x1, Pallas kernels, on_device(): pl.pallas_call(functools.partial(chain_kernel, sizes), out_shape=(pltpu.V...  61.9 us
    pallas_call x1, Pallas kernels, on_device(): pl.pallas_call(store_kernel, out_shape=tuple((pltpu.HBM(r.shape, r.dtype)...  2.47 us

profile of v4, /device:TPU:0, one launch (start us, length us, event | category | flops | bytes accessed | tf_op | source)
XLA Modules:
  0.0 65.0 jit_solution(1730758116047851025)
XLA Ops:
  0.6 61.9 %shard_map.138 = (bf16[8,1024]{1,0:T(8,128)(2,1)S(1)}, f32[4,6400]{1,0:T(4,128)S(1)}, f32[1600,512]{1,0:T(8,128)S(1)}, f32[512,1024]{1,0:T(8,128)S(1)}) custom-call(s32[4]{0:T(128)} %counts_hbm.1, s32[4]{0:T(128)} %order_hbm.1, bf16[4,6400]{1,0:T(4,128)(2,1)} %images_hbm.1, f32[6400]{0:T(1024)} %gain_hbm.1, bf16[8,1024]{1,0:T(8,128)(2,1)} %cot_hbm.1, ...), custom_call_target="tpu_custom_call" | custom-call | tf_op jit(solution)/shard_map/pallas_call | solution.py:476
  62.5 2.5 %shard_map.139 = (bf16[8,1024]{1,0:T(8,128)(2,1)}, f32[4,6400]{1,0:T(4,128)}, f32[1600,512]{1,0:T(8,128)}, f32[512,1024]{1,0:T(8,128)}) custom-call(bf16[8,1024]{1,0:T(8,128)(2,1)S(1)} %get-tuple-element.8.refs_0_, f32[4,6400]{1,0:T(4,128)S(1)} %get-tuple-element.9.refs_1_, f32[1600,512]{1,0:T(8,128)S(1)} %get-tuple-element.10.refs_2_, ...), custom_call_target="tpu_custom_call" | custom-call | tf_op jit(solution)/shard_map/pallas_call | solution.py:546
